TPU v7x, 512 devices: a whole 4x4x16 slice. The times are simulated.
512 devices in a mesh: rep: 16 (over z), ctx: 32 (over x, y, core).
Axes of the slice: x: 4, y: 4, z: 16, core: 2. Of those that a mesh axis runs over, the one named last changes fastest.
Arguments:
- query_rows: bfloat16 [16, 4096, 32, 128], P('rep', 'ctx'), may hold values from -17 to 17
- key_rows: bfloat16 [16, 4096, 4, 128], P('rep', 'ctx'), may hold values from -17 to 17
- value_matrix: bfloat16 [16, 4096, 4, 128], P('rep', 'ctx'), may hold values from -6 to 6
- cotangent: bfloat16 [16, 4096, 32, 128], P('rep', 'ctx'), may hold values from -6 to 6
- rotation: bfloat16 [16, 4, 32, 128], replicated, may hold values from -0.29882812 to 0.29882812
- projection: bfloat16 [16, 4, 32, 128], replicated, may hold values from -0.29882812 to 0.29882812
- shift_bias: float32 [16, 4], replicated, may hold values from -4 to 4
- doc_starts: int32 [16, 4096], P('rep'), may hold values from 0 to 4094, as said below
- tenant_ids: int32 [16, 4096], P('rep'), may hold values from 0 to 15, as said below
Outputs:
- d_queries: bfloat16 [16, 4096, 32, 128], P('rep', 'ctx')
- d_keys: bfloat16 [16, 4096, 4, 128], P('rep', 'ctx')
- d_values: bfloat16 [16, 4096, 4, 128], P('rep', 'ctx')
- grad_rotation: float32 [16, 4, 32, 128], P('rep', None, 'ctx')
- grad_projection: float32 [16, 4, 32, 128], P('rep', None, 'ctx')
Inputs may be any that keep to these rules, and one draw needn't show every extreme that they name: doc_starts[r, i] is the first position of the document holding position i of sequence r; documents are consecutive, each of even length 2 to 256; every sequence begins with one of exactly 256 and ends with one of length 2. `tenant_ids`: the tenant of a position's document: equal for all positions of one document.
All inputs are finite; a program needn't handle non-finite values.
Results may differ from a plain program's by a relative error of at most 0.03.
Values may be sent and summed in bfloat16 or wider, within the bound.
A program may use at most 128 MiB of HBM per device.

v0:
```python
import jax
import jax.numpy as jnp
from jax import lax
from jax.sharding import PartitionSpec as P

DOC_MAX = 256


far_below = -1e30


def shifted(value, axis, steps):
    count = lax.axis_size(axis)
    first, last = (max(0, -steps), min(count, count - steps))
    return lax.ppermute(value, axis, [(source, source + steps) for source in range(first, last)])


def tenant_terms(hidden, upstream, owners, rotation, projection):
    tenant_count = rotation.shape[0]
    low_rank = rotation.shape[1]
    tenant_mask = (jnp.arange(tenant_count, dtype=jnp.int32)[:, None] == owners[None, :]).astype(
        jnp.float32
    )
    both_maps = jnp.concatenate([projection, rotation], axis=1)
    on_both = jnp.einsum("shd,trhd->trs", hidden, both_maps, preferred_element_type=jnp.float32)
    pulled_all = jnp.einsum("shd,trhd->trs", upstream, rotation, preferred_element_type=jnp.float32)
    local_lift = jnp.sum(on_both[:, :low_rank] * tenant_mask[:, None, :], axis=0) - jnp.sum(
        on_both[:, low_rank:] * tenant_mask[:, None, :], axis=0
    )
    local_pull = jnp.sum(pulled_all * tenant_mask[:, None, :], axis=0)
    return (tenant_mask, local_lift, local_pull)


def tenant_grads(hidden, upstream, owners, tenant_count, lifted_low, pulled_low):
    mask_low = (jnp.arange(tenant_count, dtype=jnp.int32)[:, None] == owners[None, :]).astype(
        jnp.bfloat16
    )
    picked_pull = mask_low[:, None, :] * pulled_low[None]
    picked_lift = mask_low[:, None, :] * lifted_low[None]
    grad_proj = jnp.einsum("trs,shd->trhd", picked_pull, hidden, preferred_element_type=jnp.float32)
    grad_rot = (
        jnp.einsum("trs,shd->trhd", picked_lift, upstream, preferred_element_type=jnp.float32)
        - grad_proj
    )
    return (grad_rot, grad_proj)


def hidden_gradient(upstream, tenant_mask, pulled_low, rotation, projection):
    picked_pull = tenant_mask.astype(jnp.bfloat16)[:, None, :] * pulled_low[None]
    hidden_grad = (
        upstream.astype(jnp.float32)
        + jnp.einsum("trs,trhd->shd", picked_pull, projection, preferred_element_type=jnp.float32)
        - jnp.einsum("trs,trhd->shd", picked_pull, rotation, preferred_element_type=jnp.float32)
    )
    return hidden_grad.astype(jnp.bfloat16)


def group_sum(head_grads, kv_count, group_size):
    rows = head_grads.shape[0]
    rounded = lax.optimization_barrier(head_grads.astype(jnp.bfloat16))
    return (
        rounded.astype(jnp.float32)
        .reshape(rows, kv_count, group_size, head_grads.shape[-1])
        .sum(axis=2)
        .astype(jnp.bfloat16)
    )


def on_device(
    query_rows,
    key_rows,
    value_matrix,
    cotangent,
    rotation,
    projection,
    shift_bias,
    doc_starts,
    tenant_ids,
):
    queries = query_rows[0]
    key_set = key_rows[0]
    value_set = value_matrix[0]
    upstream = cotangent[0]
    starts_all = doc_starts[0]
    owners_all = tenant_ids[0]
    head_count = queries.shape[1]
    kv_count = key_set.shape[1]
    group_size = head_count // kv_count
    head_dim = queries.shape[2]
    tokens_here = queries.shape[0]
    scaling = head_dim ** (-0.5)
    tenant_count = rotation.shape[0]
    reach = (DOC_MAX + tokens_here - 1) // tokens_here
    key_parts = []
    value_parts = []
    for step in range(reach, 0, -1):
        behind_keys, behind_values = shifted((key_set, value_set), "ctx", step)
        key_parts.append(behind_keys)
        value_parts.append(behind_values)
    window_keys = jnp.concatenate(key_parts + [key_set], axis=0)
    window_values = jnp.concatenate(value_parts + [value_set], axis=0)
    row_first = lax.axis_index("ctx") * tokens_here
    starts = lax.dynamic_slice_in_dim(starts_all, row_first, tokens_here, 0)
    owners = lax.dynamic_slice_in_dim(owners_all, row_first, tokens_here, 0)
    query_place = row_first + jnp.arange(tokens_here, dtype=jnp.int32)
    key_place = (
        row_first - reach * tokens_here + jnp.arange((reach + 1) * tokens_here, dtype=jnp.int32)
    )
    allowed = (key_place[None, :] >= starts[:, None]) & (key_place[None, :] <= query_place[:, None])

    def head_scores(query_one, key_one):
        scores = (
            jnp.einsum("qgd,pd->gqp", query_one, key_one, preferred_element_type=jnp.float32)
            * scaling
        )
        return jnp.where(allowed[None], scores, far_below)

    def forward_one(pieces):
        query_one, key_one, value_one = pieces
        scores = head_scores(query_one, key_one)
        row_max = jnp.max(scores, axis=-1)
        weights = jnp.exp(scores - row_max[..., None])
        row_total = jnp.sum(weights, axis=-1)
        weights_low = (weights / row_total[..., None]).astype(jnp.bfloat16)
        hidden_one = jnp.einsum(
            "gqp,pd->qgd", weights_low, value_one, preferred_element_type=jnp.float32
        ).astype(jnp.bfloat16)
        return (hidden_one, row_max, row_total)

    query_heads = jnp.moveaxis(queries.reshape(tokens_here, kv_count, group_size, head_dim), 1, 0)
    key_heads = jnp.moveaxis(window_keys, 1, 0)
    value_heads = jnp.moveaxis(window_values, 1, 0)
    hidden_heads, maxima, totals = lax.map(forward_one, (query_heads, key_heads, value_heads))
    hidden = jnp.moveaxis(hidden_heads, 0, 1).reshape(tokens_here, head_count, head_dim)
    tenant_mask, local_lift, local_pull = tenant_terms(
        hidden, upstream, owners, rotation, projection
    )
    bias_rows = jnp.sum(shift_bias[:, :, None] * tenant_mask[:, None, :], axis=0)
    lifted_low = (local_lift + bias_rows).astype(jnp.bfloat16)
    pulled_low = local_pull.astype(jnp.bfloat16)
    grad_hidden = hidden_gradient(upstream, tenant_mask, pulled_low, rotation, projection)
    head_hidden, head_upstream = (
        lax.all_to_all(hidden, "ctx", split_axis=1, concat_axis=0, tiled=True),
        lax.all_to_all(upstream, "ctx", split_axis=1, concat_axis=0, tiled=True),
    )
    all_lift, all_pull = (
        lax.all_gather(lifted_low, "ctx", axis=1, tiled=True),
        lax.all_gather(pulled_low, "ctx", axis=1, tiled=True),
    )
    grad_rot, grad_proj = tenant_grads(
        head_hidden, head_upstream, owners_all, tenant_count, all_lift, all_pull
    )
    row_delta = jnp.sum(grad_hidden.astype(jnp.float32) * hidden.astype(jnp.float32), axis=-1)
    delta_heads = jnp.moveaxis(row_delta.reshape(tokens_here, kv_count, group_size), 0, 2)
    grad_heads = jnp.moveaxis(
        grad_hidden.reshape(tokens_here, kv_count, group_size, head_dim), 1, 0
    )

    def backward_one(pieces):
        query_one, key_one, value_one, grad_one, delta_one, row_max, row_total = pieces
        scores = head_scores(query_one, key_one)
        weights = jnp.exp(scores - row_max[..., None]) / row_total[..., None]
        weights_low = weights.astype(jnp.bfloat16)
        weight_grad = jnp.einsum(
            "qgd,pd->gqp", grad_one, value_one, preferred_element_type=jnp.float32
        )
        score_grad = (weights * (weight_grad - delta_one[:, :, None])).astype(jnp.bfloat16)
        query_grad = (
            jnp.einsum("gqp,pd->qgd", score_grad, key_one, preferred_element_type=jnp.float32)
            * scaling
        ).astype(jnp.bfloat16)
        key_grad = (
            jnp.einsum("gqp,qgd->pgd", score_grad, query_one, preferred_element_type=jnp.float32)
            * scaling
        )
        value_grad = jnp.einsum(
            "gqp,qgd->pgd", weights_low, grad_one, preferred_element_type=jnp.float32
        )
        return (query_grad, key_grad, value_grad)

    query_grads, key_grads, value_grads = lax.map(
        backward_one, (query_heads, key_heads, value_heads, grad_heads, delta_heads, maxima, totals)
    )
    own_dq = jnp.moveaxis(query_grads, 0, 1).reshape(tokens_here, head_count, head_dim)
    window_dk = jnp.moveaxis(key_grads, 0, 1).reshape(
        (reach + 1) * tokens_here, head_count, head_dim
    )
    window_dv = jnp.moveaxis(value_grads, 0, 1).reshape(
        (reach + 1) * tokens_here, head_count, head_dim
    )
    own_dk = window_dk[reach * tokens_here :]
    own_dv = window_dv[reach * tokens_here :]
    for step in range(1, reach + 1):
        lower = (reach - step) * tokens_here
        back_dk, back_dv = shifted(
            (window_dk[lower : lower + tokens_here], window_dv[lower : lower + tokens_here]),
            "ctx",
            -step,
        )
        own_dk = own_dk + back_dk
        own_dv = own_dv + back_dv
    d_keys = group_sum(own_dk, kv_count, group_size)
    d_values = group_sum(own_dv, kv_count, group_size)
    grad_rotation, grad_projection = (
        lax.psum_scatter(grad_rot, "rep", scatter_dimension=0, tiled=True),
        lax.psum_scatter(grad_proj, "rep", scatter_dimension=0, tiled=True),
    )
    return (own_dq[None], d_keys[None], d_values[None], grad_rotation, grad_projection)


def solution(mesh):
    in_specs = (
        P("rep", "ctx", None, None),
        P("rep", "ctx", None, None),
        P("rep", "ctx", None, None),
        P("rep", "ctx", None, None),
        P(),
        P(),
        P(),
        P("rep", None),
        P("rep", None),
    )
    out_specs = (
        P("rep", "ctx", None, None),
        P("rep", "ctx", None, None),
        P("rep", "ctx", None, None),
        P("rep", None, "ctx", None),
        P("rep", None, "ctx", None),
    )
    return jax.shard_map(
        on_device, mesh=mesh, in_specs=in_specs, out_specs=out_specs, check_vma=False
    )
```

profile of v0, /device:TPU:2, one launch (start us, length us, event | category | flops | bytes accessed | tf_op | source)
XLA Modules:
  0.0 463.0 jit_solution(4540721086365666059)
XLA Ops:
  10.7 3.5 collective-permute-start.2
  15.8 3.4 collective-permute-start.1
  19.2 3.2 collective-permute-start
  22.4 2.7 copy.77
  25.1 7.2 %all-to-all-start = ((bf16[128,32,128]{0,2,1:T(8,128)(2,1)}), bf16[128,32,128]{0,2,1:T(8,128)(2,1)}, u32[]{:S(2)}, u32[]{:S(2)}) async-start(bf16[128,32,128]{0,2,1:T(8,128)(2,1)} %bitcast.10), calls=%async_computation | async-start | bytes 2097152 | tf_op jit(solution)/shard_map/all_to_all | solution.py:144
  41.7 16.3 %while.30 = (s32[]{:T(128)}, bf16[4,128,8,128]{1,3,2,0:T(8,128)(2,1)}, f32[4,8,128]{2,1,0:T(8,128)}, f32[4,8,128]{2,1,0:T(8,128)}, bf16[4,384,128]{2,1,0:T(8,128...) while((s32[]{:T(128)}, ...), condition=%wide.region_4.5_spmd.clone, body=%wide.region_1.0_spmd.clone.sunk | while | flops 204748800 | bytes 5579385 | solution.py:133
  43.2 2.0 fusion.109
  47.2 2.0 fusion.109
  51.3 2.0 fusion.109
  58.0 4.3 multiply_reduce_fusion
  64.1 30.9 %while.31 = (s32[]{:T(128)}, bf16[4,128,8,128]{1,3,2,0:T(8,128)(2,1)S(1)}, f32[4,384,8,128]{1,3,2,0:T(8,128)}, f32[4,384,8,128]{1,3,2,0:T(8,128)}, bf16[4,384,12...) while((s32[]{:T(128)}, ...), condition=%wide.region_7.8_spmd.clone, body=%wide.region_6.7_spmd.clone.sunk | while | flops 507265024 | bytes 11972253 | solution.py:181
  95.1 6.3 %fusion.81 = (f32[128,4,8,128]{0,3,2,1:T(8,128)}, f32[128,4,8,128]{0,3,2,1:T(8,128)}, f32[128,4,8,128]{0,3,2,1:T(8,128)}) fusion(f32[384,4,8,128]{0,3,2,1:T(8,128)} %bitcast.240), kind=kLoop, calls=%fused_computation.121 | loop fusion | bytes 12582912 | tf_op jit(solution)/shard_map/slice | solution.py:192
  101.4 4.6 collective-permute-start.7
  106.0 2.2 collective-permute-start.6
  108.3 3.0 fusion.82
  111.2 2.6 collective-permute-start.5
  113.8 2.3 collective-permute-start.4
  116.1 8.1 %all-to-all-start.1 = ((bf16[128,32,128]{0,2,1:T(8,128)(2,1)}), bf16[128,32,128]{0,2,1:T(8,128)(2,1)S(1)}, u32[]{:S(2)}, u32[]{:S(2)}) async-start(bf16[128,32,128]{0,2,1:T(8,128)(2,1)} %bitcast.24), calls=%async_computation.1 | async-start | bytes 2097152 | tf_op jit(solution)/shard_map/all_to_all | solution.py:143
  127.0 149.8 %all_gather.7 = bf16[4,4096]{1,0:T(4,128)(2,1)S(1)} all-gather(bf16[4,128]{1,0:T(4,128)(2,1)S(1)} %copy-done.11), channel_id=1, replica_groups=mesh['rep'=16,'ctx'=32] {'ctx'}, dimensions={1}, use_global_device_ids=true | all-gather | bytes 33792 | tf_op jit(solution)/shard_map/all_gather | solution.py:148
  278.9 20.7 %all_gather.6 = bf16[4,4096]{1,0:T(4,128)(2,1)S(1)} all-gather(bf16[4,128]{1,0:T(4,128)(2,1)S(1)} %add_convert_fusion), channel_id=1, replica_groups=mesh['rep'=16,'ctx'=32] {'ctx'}, dimensions={1}, use_global_device_ids=true | all-gather | bytes 33792 | tf_op jit(solution)/shard_map/all_gather | solution.py:147
  299.6 2.3 copy.89
  310.6 135.5 %all-reduce.5.cloned.1.call-done = (f32[16,4,1,128]{3,1,2,0:T(4,128)}, f32[16,4,1,128]{3,1,2,0:T(4,128)}) async-done(((f32[16,4,1,128]{3,1,2,0:T(4,128)}, f32[16,4,1,128]{3,1,2,0:T(4,128)}), (f32[16,4,1,128]{3,1,2,0:T(4,128)}, f32[16,4,1,128]{3,1,2,0:T(4,128)})) %all-reduce.5.cloned.1.call-update) | async-done | bytes 65552
  448.1 3.4 fusion.44
  452.5 2.7 fusion.46
  (131 shorter events, 74.5 us)
Async XLA Ops:
  7.2 28.3 %copy-start = (s32[1,4096]{1,0:T(1,128)S(1)}, s32[1,4096]{1,0:T(1,128)}, u32[]{:S(2)}) copy-start(s32[1,4096]{1,0:T(1,128)} %param.20) | copy-start | bytes 49156
  8.8 28.8 %collective-permute-start.3 = (bf16[128,4,128]{2,0,1:T(8,128)(2,1)}, bf16[128,4,128]{2,0,1:T(8,128)(2,1)}, u32[]{:S(2)}, u32[]{:S(2)}) collective-permute-start(bf16[128,4,128]{2,0,1:T(8,128)(2,1)} %bitcast.194), channel_id=1, source_target_pairs={{0,1},{1,2},{2,3},{3,4},{4,5},{5,6},{6,7},{7,8},{8,9},{9,10},{10,1... | collective-permute-start | bytes 393224 | tf_op jit(solution)/shard_map/ppermute | solution.py:15
  10.7 26.9 %collective-permute-start.2 = (bf16[128,4,128]{2,0,1:T(8,128)(2,1)}, bf16[128,4,128]{2,0,1:T(8,128)(2,1)}, u32[]{:S(2)}, u32[]{:S(2)}) collective-permute-start(bf16[128,4,128]{2,0,1:T(8,128)(2,1)} %bitcast.194), channel_id=1, source_target_pairs={{0,2},{1,3},{2,4},{3,5},{4,6},{5,7},{6,8},{7,9},{8,10},{9,11},{10,... | collective-permute-start | bytes 393224 | tf_op jit(solution)/shard_map/ppermute | solution.py:15
  15.8 17.8 %copy-start.4 = (bf16[16,4,32,128]{3,2,1,0:T(8,128)(2,1)S(1)}, bf16[16,4,32,128]{3,2,1,0:T(8,128)(2,1)}, u32[]{:S(2)}) copy-start(bf16[16,4,32,128]{3,2,1,0:T(8,128)(2,1)} %param.17) | copy-start | bytes 1572868
  15.8 17.8 %copy-start.5 = (bf16[1,128,32,128]{3,2,1,0:T(8,128)(2,1)S(1)}, bf16[1,128,32,128]{3,2,1,0:T(8,128)(2,1)}, u32[]{:S(2)}) copy-start(bf16[1,128,32,128]{3,2,1,0:T(8,128)(2,1)} %param.16) | copy-start | bytes 3145732
  15.8 23.7 %collective-permute-start.1 = (bf16[128,4,128]{2,0,1:T(8,128)(2,1)}, bf16[128,4,128]{2,0,1:T(8,128)(2,1)}, u32[]{:S(2)}, u32[]{:S(2)}) collective-permute-start(bf16[128,4,128]{2,0,1:T(8,128)(2,1)} %bitcast.195), channel_id=1, source_target_pairs={{0,1},{1,2},{2,3},{3,4},{4,5},{5,6},{6,7},{7,8},{8,9},{9,10},{10,1... | collective-permute-start | bytes 393224 | tf_op jit(solution)/shard_map/ppermute | solution.py:15
  19.2 20.3 %collective-permute-start = (bf16[128,4,128]{2,0,1:T(8,128)(2,1)}, bf16[128,4,128]{2,0,1:T(8,128)(2,1)}, u32[]{:S(2)}, u32[]{:S(2)}) collective-permute-start(bf16[128,4,128]{2,0,1:T(8,128)(2,1)} %bitcast.195), channel_id=1, source_target_pairs={{0,2},{1,3},{2,4},{3,5},{4,6},{5,7},{6,8},{7,9},{8,10},{9,11},{10,... | collective-permute-start | bytes 393224 | tf_op jit(solution)/shard_map/ppermute | solution.py:15
  25.1 9.2 %copy-start.3 = (bf16[16,4,32,128]{3,2,1,0:T(8,128)(2,1)S(1)}, bf16[16,4,32,128]{3,2,1,0:T(8,128)(2,1)}, u32[]{:S(2)}) copy-start(bf16[16,4,32,128]{3,2,1,0:T(8,128)(2,1)} %param.18) | copy-start | bytes 1572868
  25.1 91.0 %all-to-all-start = ((bf16[128,32,128]{0,2,1:T(8,128)(2,1)}), bf16[128,32,128]{0,2,1:T(8,128)(2,1)}, u32[]{:S(2)}, u32[]{:S(2)}) async-start(bf16[128,32,128]{0,2,1:T(8,128)(2,1)} %bitcast.10), calls=%async_computation | async-start | bytes 2097152 | tf_op jit(solution)/shard_map/all_to_all | solution.py:144
  33.5 1.3 copy-start.7
  95.1 6.3 %copy-start.1 = (bf16[4,128,8,128]{1,3,2,0:T(8,128)(2,1)}, bf16[4,128,8,128]{1,3,2,0:T(8,128)(2,1)S(1)}, u32[]{:S(2)}) copy-start(bf16[4,128,8,128]{1,3,2,0:T(8,128)(2,1)S(1)} %get-tuple-element.116) | copy-start | bytes 3145732
  95.1 13.1 %slice-start = ((s8[6291456]{0:T(1024)(128)(4,1)}), s8[4194304]{0:T(1024)(128)(4,1)S(1)}, s32[]{:S(2)}) async-start(s8[6291456]{0:T(1024)(128)(4,1)} %bitcast.241), calls=%async_computation.3 | async-start | bytes 8388608
  95.1 13.1 %slice-start.1 = ((s8[6291456]{0:T(1024)(128)(4,1)}), s8[2097152]{0:T(1024)(128)(4,1)S(1)}, s32[]{:S(2)}) async-start(s8[6291456]{0:T(1024)(128)(4,1)} %bitcast.241), calls=%async_computation.4 | async-start | bytes 4194304
  101.4 346.7 %collective-permute-start.7 = (f32[128,32,128]{0,2,1:T(8,128)}, f32[128,32,128]{0,2,1:T(8,128)}, u32[]{:S(2)}, u32[]{:S(2)}) collective-permute-start(f32[128,32,128]{0,2,1:T(8,128)} %bitcast.38), channel_id=1, source_target_pairs={{2,0},{3,1},{4,2},{5,3},{6,4},{7,5},{8,6},{9,7},{10,8},{11,9},{12,... | collective-permute-start | bytes 6291464 | tf_op jit(solution)/shard_map/ppermute | solution.py:15
  106.0 342.1 %collective-permute-start.6 = (f32[128,32,128]{0,2,1:T(8,128)}, f32[128,32,128]{0,2,1:T(8,128)}, u32[]{:S(2)}, u32[]{:S(2)}) collective-permute-start(f32[128,32,128]{0,2,1:T(8,128)} %bitcast.37), channel_id=1, source_target_pairs={{1,0},{2,1},{3,2},{4,3},{5,4},{6,5},{7,6},{8,7},{9,8},{10,9},{11,1... | collective-permute-start | bytes 6291464 | tf_op jit(solution)/shard_map/ppermute | solution.py:15
  111.2 13.1 %copy-start.9 = (s32[1,4096]{1,0:T(1,128)S(1)}, s32[1,4096]{1,0:T(1,128)}, u32[]{:S(2)}) copy-start(s32[1,4096]{1,0:T(1,128)} %param.21) | copy-start | bytes 49156
  111.2 341.3 %collective-permute-start.5 = (f32[128,32,128]{0,2,1:T(8,128)}, f32[128,32,128]{0,2,1:T(8,128)}, u32[]{:S(2)}, u32[]{:S(2)}) collective-permute-start(f32[128,32,128]{0,2,1:T(8,128)} %bitcast.32), channel_id=1, source_target_pairs={{2,0},{3,1},{4,2},{5,3},{6,4},{7,5},{8,6},{9,7},{10,8},{11,9},{12,... | collective-permute-start | bytes 6291464 | tf_op jit(solution)/shard_map/ppermute | solution.py:15
  113.8 338.7 %collective-permute-start.4 = (f32[128,32,128]{0,2,1:T(8,128)}, f32[128,32,128]{0,2,1:T(8,128)}, u32[]{:S(2)}, u32[]{:S(2)}) collective-permute-start(f32[128,32,128]{0,2,1:T(8,128)} %bitcast.31), channel_id=1, source_target_pairs={{1,0},{2,1},{3,2},{4,3},{5,4},{6,5},{7,6},{8,7},{9,8},{10,9},{11,1... | collective-permute-start | bytes 6291464 | tf_op jit(solution)/shard_map/ppermute | solution.py:15
  116.1 10.9 %copy-start.11 = (bf16[4,128]{1,0:T(4,128)(2,1)S(1)}, bf16[4,128]{1,0:T(4,128)(2,1)}, u32[]{:S(2)}) copy-start(bf16[4,128]{1,0:T(4,128)(2,1)} %copy-done.10) | copy-start | bytes 3076
  116.1 185.7 %all-to-all-start.1 = ((bf16[128,32,128]{0,2,1:T(8,128)(2,1)}), bf16[128,32,128]{0,2,1:T(8,128)(2,1)S(1)}, u32[]{:S(2)}, u32[]{:S(2)}) async-start(bf16[128,32,128]{0,2,1:T(8,128)(2,1)} %bitcast.24), calls=%async_computation.1 | async-start | bytes 2097152 | tf_op jit(solution)/shard_map/all_to_all | solution.py:143
  124.3 321.9 %all-reduce.5.cloned.1.call-start = ((), (), s32[]{:S(2)}) async-start(), calls=%async_computation.2 | async-start | bytes 131072
  127.0 151.8 %copy-start.8 = (f32[16,128]{1,0:T(8,128)S(1)}, f32[16,128]{1,0:T(8,128)}, u32[]{:S(2)}) copy-start(f32[16,128]{1,0:T(8,128)} %copy-done.7) | copy-start | bytes 24580
  127.0 151.8 %copy-start.12 = (f32[16,4]{0,1:T(4,128)S(1)}, f32[16,4]{0,1:T(4,128)}, u32[]{:S(2)}) copy-start(f32[16,4]{0,1:T(4,128)} %param.19) | copy-start | bytes 772
  303.2 5.8 %copy-start.2 = (bf16[4,128,8,128]{1,3,2,0:T(8,128)(2,1)S(1)}, bf16[4,128,8,128]{1,3,2,0:T(8,128)(2,1)}, u32[]{:S(2)}) copy-start(bf16[4,128,8,128]{1,3,2,0:T(8,128)(2,1)} %copy-done.1) | copy-start | bytes 3145732
  (2 other events, 2.5 us)
Sparse Core Ops, SparseCore 0:
  307.7 138.3 all-reduce.4
where the time goes:
time: 465 us; the launch traced here: 463 us
  blocking collectives  171 us (37%)
  waiting for transfers between devices  136 us (29%)
  local copies, waits for them, and re-layouts  42.9 us (9%)
  matrix products  42.3 us (9%)
  starting transfers between devices  39.1 us (8%)
  other arithmetic  17.9 us (4%)
  between operations  14.4 us (3%)
    all_gather x1, blocking collectives, on_device(): lax.all_gather(pulled_low, 'ctx', axis=1, tiled=True)  150 us
    unnamed x2, waiting for transfers between devices  136 us
    ppermute x8, starting transfers between devices, shifted(): lax.ppermute(value, axis, [(source, source + steps) for source in range(f...  23.7 us
    all_gather x1, blocking collectives, on_device(): lax.all_gather(lifted_low, 'ctx', axis=1, tiled=True)  20.7 us
    unnamed x40, local copies, waits for them, and re-layouts  15.1 us
  transfers between devices with their start and end apart: 11, of which 1 were waited for; matrix products, arithmetic and copies ran while one was open for 21% of the time, Pallas kernels for 0%

commit v1 on v0

v1 whole, which is shorter than its diff:
```python
import jax
import jax.numpy as jnp
from jax import lax
from jax.experimental import pallas as pl
from jax.experimental.pallas import tpu as pltpu
from jax.sharding import PartitionSpec as P_

f32, bf16 = jnp.float32, jnp.bfloat16
MESH = pl.DeviceIdType.MESH
LOG2E = 1.4426950408889634


def dot(a, b):
    return jnp.dot(a, b, preferred_element_type=f32)


def dot_nt(a, b):
    return lax.dot_general(a, b, (((1,), (1,)), ((), ())), preferred_element_type=f32)


def iota(shape, d):
    return lax.broadcasted_iota(jnp.int32, shape, d)


def stage_prep(q_ref, c_ref, w_ref, r_ref, Q, C2, WR):
    for m in range(4):
        Q[m] = jnp.swapaxes(q_ref[:, 8 * m : 8 * m + 8, :], 0, 1).reshape(1024, 128)
    C2[...] = c_ref[...].reshape(128, 4096)
    WR[0:64] = w_ref[...].reshape(64, 4096)
    WR[64:128] = r_ref[...].reshape(64, 4096)


def stage_mask(starts, row_first, MB):
    key_place = row_first - 256 + iota((384, 128), 0)
    query_place = row_first + iota((384, 128), 1)
    allowed = (key_place >= starts) & (key_place <= query_place)
    MB[...] = jnp.where(allowed, 0.0, -1e30).astype(f32)


def stage_fwd(m, KV, Q, MB, P, HT, scale):
    vt = KV[m, 1].T
    st = dot_nt(KV[m, 0], Q[m])
    s = st * (scale * LOG2E) + jnp.concatenate([MB[...]] * 8, axis=1)
    e = jnp.exp2(s - jnp.max(s, axis=0, keepdims=True))
    wl = (e * (1.0 / jnp.sum(e, axis=0, keepdims=True))).astype(bf16)
    P[m] = wl
    ht = dot(vt, wl).astype(bf16)
    for g in range(8):
        HT[pl.ds(m * 1024 + g * 128, 128), :] = ht[:, g * 128 : (g + 1) * 128]


def stage_pull(own, WR, C2, GH, PL):
    mask = iota((64, 128), 0) // 4 == own
    pull = jnp.where(mask, dot_nt(WR[64:128], C2[...]), 0.0)
    PL[...] = pull.astype(bf16)
    pt = jnp.concatenate([pull, -pull], axis=0).T.astype(bf16)
    for m in range(4):
        cols = slice(m * 1024, (m + 1) * 1024)
        gh = (dot(pt, WR[:, cols]) + C2[:, cols].astype(f32)).astype(bf16)
        for g in range(8):
            GH[m, g * 128 : (g + 1) * 128, :] = gh[:, g * 128 : (g + 1) * 128]


def stage_tenant(own, bias_sm, WR, C2, HT, PL, G, send):
    mask = iota((64, 128), 0) // 4 == own
    lift2 = dot(WR[...], HT[...])
    ridx = iota((8, 128), 0)
    shifts = []
    for b in range(8):
        a = jnp.zeros((8, 128), f32)
        for r in range(8):
            a = jnp.where(ridx == r, bias_sm[(b * 8 + r) // 4, r % 4], a)
        shifts.append(a)
    lift = lift2[0:64] - lift2[64:128] + jnp.concatenate(shifts, axis=0)
    lift = jnp.where(mask, lift, 0.0).astype(bf16)
    r = iota((128, 64), 0)
    c = iota((128, 64), 1)
    hit = c == (r // 8) * 4 + r % 4
    first = (r // 4) % 2 == 0
    li = dot(jnp.where(hit & first, 1.0, 0.0).astype(bf16), lift).astype(bf16)
    pi = dot(jnp.where(hit, jnp.where(first, -1.0, 1.0), 0.0).astype(bf16), PL[...]).astype(bf16)
    for m in range(4):
        part = dot(li, C2[:, m * 1024 : (m + 1) * 1024])
        part = part + dot_nt(pi, HT[m * 1024 : (m + 1) * 1024, :])
        part = part.astype(bf16)
        for g in range(8):
            G[g % 2, m * 4 + g // 2] = part[:, g * 128 : (g + 1) * 128]
        send(m)


def stage_bwd(m, KV, Q, P, GH, scale, DQ, SB, OWN):
    kt = KV[m, 0].T
    gh = GH[m]
    dp = dot_nt(KV[m, 1], gh)
    wl = P[m]
    w = wl.astype(f32)
    wd = w * dp
    delta = jnp.sum(wd, axis=0, keepdims=True)
    ds = (wd - w * delta).astype(bf16)
    dk = dot(ds, Q[m]) * scale
    dv = dot(wl, gh)
    for s in (1, 2):
        rows = slice(HALO - 128 * s, HALO - 128 * s + 128)
        SB[m, s - 1, 0] = dk[rows].astype(bf16)
        SB[m, s - 1, 1] = dv[rows].astype(bf16)
    OWN[m, 0] = dk[HALO:]
    OWN[m, 1] = dv[HALO:]
    dqt = dot(kt, ds) * scale
    for g in range(8):
        DQ[m * 8 + g] = dqt[:, g * 128 : (g + 1) * 128].T.astype(bf16)


REPS, CTXS, CHIPS = 16, 32, 16
HALO = 256


def kernel(
    q_hbm, c_hbm, k_hbm, v_hbm, w_hbm, r_hbm, bias_sm, starts_ref, owners_ref,
    dq_ref, dk_ref, dv_ref, gr_ref, gp_ref,
    q_in, c_in, k_in, v_in, w_in, r_in, in_sem,
    KV, Q, C2, WR, MB, P, HT, GH, DQ, PL,
    halo_send, halo_recv,
    SB, RB, OWN, back_send, back_recv,
    G, R1, one_send, one_recv,
    S2, R2, two_send, two_recv,
    S3, R3, three_send, three_recv,
):
    rep = lax.axis_index("rep")
    ctx = lax.axis_index("ctx")
    chip = ctx // 2
    core = ctx % 2
    mate = ctx + 1 - 2 * core
    scale = 128 ** -0.5

    def there(x):
        return (rep, x)

    loads = []
    for i, (src, dst) in enumerate(
        ((k_hbm, k_in), (v_hbm, v_in), (q_hbm, q_in), (c_hbm, c_in), (w_hbm, w_in), (r_hbm, r_in))
    ):
        cp = pltpu.make_async_copy(src, dst, in_sem.at[i])
        cp.start()
        loads.append(cp)

    barrier = pltpu.get_barrier_semaphore()
    for d in (1, CTXS - 1):
        pl.semaphore_signal(barrier, inc=1, device_id=there((ctx + d) % CTXS), device_id_type=MESH)
    for d in range(1, CHIPS):
        pl.semaphore_signal(
            barrier, inc=1, device_id=there((ctx + 2 * d) % CTXS), device_id_type=MESH
        )
    for d in range(1, REPS):
        pl.semaphore_signal(
            barrier, inc=1, device_id=((rep + d) % REPS, ctx), device_id_type=MESH
        )

    loads[0].wait()
    loads[1].wait()
    kk = jnp.swapaxes(k_in[...].astype(f32), 0, 1).astype(bf16)
    vv = jnp.swapaxes(v_in[...].astype(f32), 0, 1).astype(bf16)
    for m in range(4):
        KV[m, 0, HALO:] = kk[m]
        KV[m, 1, HALO:] = vv[m]
    loads[2].wait()
    loads[3].wait()
    loads[4].wait()
    loads[5].wait()
    stage_prep(q_in, c_in, w_in, r_in, Q, C2, WR)
    row_first = ctx * 128
    lanes = pl.ds(pl.multiple_of(row_first, 128), 128)
    own = owners_ref[:, lanes]
    stage_mask(starts_ref[:, lanes], row_first, MB)

    pl.semaphore_wait(barrier, 2 + (CHIPS - 1) + (REPS - 1))

    def halo_copy(m, s):
        return pltpu.make_async_remote_copy(
            src_ref=KV.at[m, :, pl.ds(HALO, 128)],
            dst_ref=KV.at[m, :, pl.ds(HALO - 128 * s, 128)],
            send_sem=halo_send.at[m, s - 1],
            recv_sem=halo_recv.at[m, s - 1],
            device_id=there((ctx + s) % CTXS),
            device_id_type=MESH,
        )

    for m in range(4):
        for s in (1, 2):
            halo_copy(m, s).start()

    stage_pull(own, WR, C2, GH, PL)

    def fwd(m, carry):
        for s in (1, 2):
            halo_copy(m, s).wait_recv()
        stage_fwd(m, KV, Q, MB, P, HT, scale)
        return carry

    lax.fori_loop(0, 4, fwd, 0)

    def one_copy(m):
        return pltpu.make_async_remote_copy(
            src_ref=G.at[1 - core, pl.ds(4 * m, 4)],
            dst_ref=R1.at[pl.ds(4 * m, 4)],
            send_sem=one_send.at[m],
            recv_sem=one_recv.at[m],
            device_id=there(mate),
            device_id_type=MESH,
        )

    def two_copy(d):
        return pltpu.make_async_remote_copy(
            src_ref=S2.at[(chip + d) % CHIPS],
            dst_ref=R2.at[d],
            send_sem=two_send.at[d],
            recv_sem=two_recv.at[d],
            device_id=there((ctx + 2 * d) % CTXS),
            device_id_type=MESH,
        )

    def three_copy(d):
        return pltpu.make_async_remote_copy(
            src_ref=S3.at[(rep + d) % REPS],
            dst_ref=R3.at[d],
            send_sem=three_send.at[d],
            recv_sem=three_recv.at[d],
            device_id=((rep + d) % REPS, ctx),
            device_id_type=MESH,
        )

    def back_copy(m, s):
        return pltpu.make_async_remote_copy(
            src_ref=SB.at[m, s - 1],
            dst_ref=RB.at[m, s - 1],
            send_sem=back_send.at[m, s - 1],
            recv_sem=back_recv.at[m, s - 1],
            device_id=there((ctx + CTXS - s) % CTXS),
            device_id_type=MESH,
        )

    stage_tenant(own, bias_sm, WR, C2, HT, PL, G, lambda m: one_copy(m).start())

    def bwd(m, carry):
        stage_bwd(m, KV, Q, P, GH, scale, DQ, SB, OWN)
        for s in (1, 2):
            back_copy(m, s).start()

        @pl.when(m == 0)
        def _():
            for i in range(4):
                one_copy(i).wait_recv()
            S2[...] = (G[core].astype(f32) + R1[...].astype(f32)).astype(bf16)
            for d in range(1, CHIPS):
                two_copy(d).start()

        @pl.when(m == 2)
        def _():
            total = S2[chip].astype(f32)
            for d in range(1, CHIPS):
                two_copy(d).wait_recv()
                total = total + R2[d].astype(f32)
            S3[...] = total.reshape(REPS, 8, 128)
            for d in range(1, REPS):
                three_copy(d).start()

        return carry

    lax.fori_loop(0, 4, bwd, 0)

    for m in range(4):
        dq_ref[:, 8 * m : 8 * m + 8, :] = jnp.swapaxes(DQ[8 * m : 8 * m + 8], 0, 1)

    mine = S3[rep]
    for d in range(1, REPS):
        three_copy(d).wait_recv()
        mine = mine + R3[d]
    gr_ref[...] = mine[0:4]
    gp_ref[...] = mine[4:8]

    for m in range(4):
        for s in (1, 2):
            back_copy(m, s).wait_recv()
    total = OWN[...] + RB[:, 0].astype(f32) + RB[:, 1].astype(f32)
    dk_ref[...] = jnp.swapaxes(total[:, 0], 0, 1).astype(bf16)
    dv_ref[...] = jnp.swapaxes(total[:, 1], 0, 1).astype(bf16)

    for m in range(4):
        one_copy(m).wait_send()
        for s in (1, 2):
            halo_copy(m, s).wait_send()
            back_copy(m, s).wait_send()
    for d in range(1, CHIPS):
        two_copy(d).wait_send()
    for d in range(1, REPS):
        three_copy(d).wait_send()


def on_device(
    query_rows, key_rows, value_matrix, cotangent, rotation, projection, shift_bias,
    doc_starts, tenant_ids,
):
    vmem = pl.BlockSpec(memory_space=pltpu.VMEM)
    smem = pl.BlockSpec(memory_space=pltpu.SMEM)
    hbm = pl.BlockSpec(memory_space=pl.ANY)
    dma = pltpu.SemaphoreType.DMA
    rows = (128, 32, 128)
    out = pl.pallas_call(
        kernel,
        out_shape=(
            jax.ShapeDtypeStruct(rows, bf16),
            jax.ShapeDtypeStruct((128, 4, 128), bf16),
            jax.ShapeDtypeStruct((128, 4, 128), bf16),
            jax.ShapeDtypeStruct((4, 128), f32),
            jax.ShapeDtypeStruct((4, 128), f32),
        ),
        in_specs=[hbm] * 6 + [smem, vmem, vmem],
        out_specs=(vmem,) * 5,
        scratch_shapes=[
            pltpu.VMEM(rows, bf16), pltpu.VMEM(rows, bf16),
            pltpu.VMEM((128, 4, 128), bf16), pltpu.VMEM((128, 4, 128), bf16),
            pltpu.VMEM((64, 32, 128), bf16), pltpu.VMEM((64, 32, 128), bf16),
            dma((6,)),
            pltpu.VMEM((4, 2, 384, 128), bf16),
            pltpu.VMEM((4, 1024, 128), bf16),
            pltpu.VMEM((128, 4096), bf16),
            pltpu.VMEM((128, 4096), bf16),
            pltpu.VMEM((384, 128), f32),
            pltpu.VMEM((4, 384, 1024), bf16),
            pltpu.VMEM((4096, 128), bf16),
            pltpu.VMEM((4, 1024, 128), bf16),
            pltpu.VMEM((32, 128, 128), bf16),
            pltpu.VMEM((64, 128), bf16),
            dma((4, 2)), dma((4, 2)),
            pltpu.VMEM((4, 2, 2, 128, 128), bf16),
            pltpu.VMEM((4, 2, 2, 128, 128), bf16),
            pltpu.VMEM((4, 2, 128, 128), f32),
            dma((4, 2)), dma((4, 2)),
            pltpu.VMEM((2, CHIPS, 128, 128), bf16),
            pltpu.VMEM((CHIPS, 128, 128), bf16),
            dma((4,)), dma((4,)),
            pltpu.VMEM((CHIPS, 128, 128), bf16),
            pltpu.VMEM((CHIPS, 128, 128), bf16),
            dma((CHIPS,)), dma((CHIPS,)),
            pltpu.VMEM((REPS, 8, 128), f32),
            pltpu.VMEM((REPS, 8, 128), f32),
            dma((REPS,)), dma((REPS,)),
        ],
        compiler_params=pltpu.CompilerParams(
            collective_id=0, has_side_effects=True, vmem_limit_bytes=48 << 20
        ),
        name="steered_attention_backward",
    )(
        query_rows[0], cotangent[0], key_rows[0], value_matrix[0],
        projection.reshape(64, 32, 128), rotation.reshape(64, 32, 128),
        shift_bias, doc_starts, tenant_ids,
    )
    dq, dk, dv, gr, gp = out
    return dq[None], dk[None], dv[None], gr.reshape(1, 4, 1, 128), gp.reshape(1, 4, 1, 128)


def solution(mesh):
    row = P_("rep", "ctx", None, None)
    in_specs = (row, row, row, row, P_(), P_(), P_(), P_("rep", None), P_("rep", None))
    grads = P_("rep", None, "ctx", None)
    return jax.shard_map(
        on_device, mesh=mesh, in_specs=in_specs, out_specs=(row, row, row, grads, grads),
        check_vma=False,
    )
```

time: 465 us -> 62.6 us (0.13)
  the two profiles are of different devices: /device:TPU:2 before, /device:TPU:30 now
where the time goes in v1:
time: 62.6 us; the launch traced here: 62.2 us
  Pallas kernels  50.2 us (80%)
  local copies, waits for them, and re-layouts  11.3 us (18%)
  between operations  0.66 us (1%)
    pallas_call x1, Pallas kernels, on_device(): pl.pallas_call(kernel, out_shape=(jax.ShapeDtypeStruct(rows, bf16), jax.S...  50.2 us
    unnamed x22, local copies, waits for them, and re-layouts  11.3 us

profile of v1, /device:TPU:30, one launch (start us, length us, event | category | flops | bytes accessed | tf_op | source)
XLA Modules:
  0.0 62.2 jit_solution(10893228460395496333)
XLA Ops:
  0.6 0.0 copy-start.6
  0.6 0.8 %copy.14.bias_sm = f32[16,4]{1,0:T(8,128)S(1)} copy(f32[16,4]{0,1:T(4,128)} %param.15) | data formatting | bytes 512 | tf_op args[6]
  1.4 0.0 copy-done.6
  1.4 0.0 copy-start
  1.4 1.2 %copy-done = bf16[1,128,32,128]{3,2,1,0:T(8,128)(2,1)S(1)} copy-done((bf16[1,128,32,128]{3,2,1,0:T(8,128)(2,1)S(1)}, bf16[1,128,32,128]{3,2,1,0:T(8,128)(2,1)}, u32[]{:S(2)}) %copy-start) | copy-done | bytes 1048600
  2.6 0.0 copy-start.1
  2.6 1.2 %copy-done.1 = bf16[1,128,32,128]{3,2,1,0:T(8,128)(2,1)S(1)} copy-done((bf16[1,128,32,128]{3,2,1,0:T(8,128)(2,1)S(1)}, bf16[1,128,32,128]{3,2,1,0:T(8,128)(2,1)}, u32[]{:S(2)}) %copy-start.1) | copy-done | bytes 1048600
  3.9 0.0 copy-start.2
  3.9 1.0 %copy-done.2 = bf16[16,4,32,128]{3,2,1,0:T(8,128)(2,1)S(1)} copy-done((bf16[16,4,32,128]{3,2,1,0:T(8,128)(2,1)S(1)}, bf16[16,4,32,128]{3,2,1,0:T(8,128)(2,1)}, u32[]{:S(2)}) %copy-start.2) | copy-done | bytes 524312
  4.9 0.0 copy-start.3
  4.9 1.0 %copy-done.3 = bf16[16,4,32,128]{3,2,1,0:T(8,128)(2,1)S(1)} copy-done((bf16[16,4,32,128]{3,2,1,0:T(8,128)(2,1)S(1)}, bf16[16,4,32,128]{3,2,1,0:T(8,128)(2,1)}, u32[]{:S(2)}) %copy-start.3) | copy-done | bytes 524312
  5.9 0.0 copy-start.4
  5.9 0.9 %copy-done.4 = bf16[1,128,4,128]{3,2,1,0:T(4,128)(2,1)S(1)} copy-done((bf16[1,128,4,128]{3,2,1,0:T(4,128)(2,1)S(1)}, bf16[1,128,4,128]{3,2,1,0:T(4,128)(2,1)}, u32[]{:S(2)}) %copy-start.4) | copy-done | bytes 131096
  6.8 0.0 copy-start.5
  6.9 0.9 %copy-done.5 = bf16[1,128,4,128]{3,2,1,0:T(4,128)(2,1)S(1)} copy-done((bf16[1,128,4,128]{3,2,1,0:T(4,128)(2,1)S(1)}, bf16[1,128,4,128]{3,2,1,0:T(4,128)(2,1)}, u32[]{:S(2)}) %copy-start.5) | copy-done | bytes 131096
  7.8 0.0 copy-start.7
  7.8 0.7 %copy-done.7 = s32[1,4096]{1,0:T(1,128)S(1)} copy-done((s32[1,4096]{1,0:T(1,128)S(1)}, s32[1,4096]{1,0:T(1,128)}, u32[]{:S(2)}) %copy-start.7) | copy-done | bytes 16408
  8.5 50.2 %steered_attention_backward.1 = (bf16[128,32,128]{2,1,0:T(8,128)(2,1)S(1)}, bf16[128,4,128]{2,1,0:T(4,128)(2,1)S(1)}, bf16[128,4,128]{2,1,0:T(4,128)(2,1)S(1)}, f32[4,128]{1,0:T(4,128)S(1)}, f32[4,128]{1,0:T(4,128)S(1)}) custom-call(bf16[128,32,128]{2,1,0:T(8,128)(2,1)S(1)} %bitcast.15, bf16[128,32,128]{2,1,0:T(8,128)(2,1)S(1)} %bitcast.16, ...), custom_call_target="tpu_custom_call" | custom-call | tf_op jit(solution)/shard_map/steered_attention_backward/pallas_call | solution.py:307
  58.7 1.0 %copy.22 = bf16[1,128,32,128]{3,2,1,0:T(8,128)(2,1)} copy(bf16[1,128,32,128]{3,2,1,0:T(8,128)(2,1)S(1)} %bitcast.17) | data formatting | bytes 2097152
  59.7 0.7 %copy.23 = bf16[1,128,4,128]{3,2,1,0:T(4,128)(2,1)} copy(bf16[1,128,4,128]{3,2,1,0:T(4,128)(2,1)S(1)} %bitcast.21) | data formatting | bytes 262144
  60.3 0.7 %copy.24 = bf16[1,128,4,128]{3,2,1,0:T(4,128)(2,1)} copy(bf16[1,128,4,128]{3,2,1,0:T(4,128)(2,1)S(1)} %bitcast.20) | data formatting | bytes 262144
  61.0 0.6 copy.25
  61.6 0.6 copy.26
Async XLA Ops:
  0.6 0.8 %copy-start.6 = (s32[1,4096]{1,0:T(1,128)S(1)}, s32[1,4096]{1,0:T(1,128)}, u32[]{:S(2)}) copy-start(s32[1,4096]{1,0:T(1,128)} %starts_ref.1) | copy-start | bytes 49156
  1.4 1.2 %copy-start = (bf16[1,128,32,128]{3,2,1,0:T(8,128)(2,1)S(1)}, bf16[1,128,32,128]{3,2,1,0:T(8,128)(2,1)}, u32[]{:S(2)}) copy-start(bf16[1,128,32,128]{3,2,1,0:T(8,128)(2,1)} %param.9) | copy-start | bytes 3145732
  2.6 1.2 %copy-start.1 = (bf16[1,128,32,128]{3,2,1,0:T(8,128)(2,1)S(1)}, bf16[1,128,32,128]{3,2,1,0:T(8,128)(2,1)}, u32[]{:S(2)}) copy-start(bf16[1,128,32,128]{3,2,1,0:T(8,128)(2,1)} %param.12) | copy-start | bytes 3145732
  3.9 1.0 %copy-start.2 = (bf16[16,4,32,128]{3,2,1,0:T(8,128)(2,1)S(1)}, bf16[16,4,32,128]{3,2,1,0:T(8,128)(2,1)}, u32[]{:S(2)}) copy-start(bf16[16,4,32,128]{3,2,1,0:T(8,128)(2,1)} %param.14) | copy-start | bytes 1572868
  4.9 1.0 %copy-start.3 = (bf16[16,4,32,128]{3,2,1,0:T(8,128)(2,1)S(1)}, bf16[16,4,32,128]{3,2,1,0:T(8,128)(2,1)}, u32[]{:S(2)}) copy-start(bf16[16,4,32,128]{3,2,1,0:T(8,128)(2,1)} %param.13) | copy-start | bytes 1572868
  5.9 0.9 %copy-start.4 = (bf16[1,128,4,128]{3,2,1,0:T(4,128)(2,1)S(1)}, bf16[1,128,4,128]{3,2,1,0:T(4,128)(2,1)}, u32[]{:S(2)}) copy-start(bf16[1,128,4,128]{3,2,1,0:T(4,128)(2,1)} %param.10) | copy-start | bytes 393220
  6.8 0.9 %copy-start.5 = (bf16[1,128,4,128]{3,2,1,0:T(4,128)(2,1)S(1)}, bf16[1,128,4,128]{3,2,1,0:T(4,128)(2,1)}, u32[]{:S(2)}) copy-start(bf16[1,128,4,128]{3,2,1,0:T(4,128)(2,1)} %param.11) | copy-start | bytes 393220
  7.8 0.7 %copy-start.7 = (s32[1,4096]{1,0:T(1,128)S(1)}, s32[1,4096]{1,0:T(1,128)}, u32[]{:S(2)}) copy-start(s32[1,4096]{1,0:T(1,128)} %owners_ref.1) | copy-start | bytes 49156

commit v2 on v1

--- a/solution.py
+++ b/solution.py
@@ -69,7 +69,7 @@
     for b in range(8):
         a = jnp.zeros((8, 128), f32)
         for r in range(8):
-            a = jnp.where(ridx == r, bias_sm[(b * 8 + r) // 4, r % 4], a)
+            a = jnp.where(ridx == r, bias_sm[r % 4, (b * 8 + r) // 4], a)
         shifts.append(a)
     lift = lift2[0:64] - lift2[64:128] + jnp.concatenate(shifts, axis=0)
     lift = jnp.where(mask, lift, 0.0).astype(bf16)
@@ -112,13 +112,15 @@
 
 REPS, CTXS, CHIPS = 16, 32, 16
 HALO = 256
+VMEM_LIMIT = 60 << 20
 
 
 def kernel(
-    q_hbm, c_hbm, k_hbm, v_hbm, w_hbm, r_hbm, bias_sm, starts_ref, owners_ref,
-    dq_ref, dk_ref, dv_ref, gr_ref, gp_ref,
-    q_in, c_in, k_in, v_in, w_in, r_in, in_sem,
-    KV, Q, C2, WR, MB, P, HT, GH, DQ, PL,
+    q_hbm, c_hbm, k_hbm, v_hbm, w_hbm, r_hbm, starts_hbm, owners_hbm, bias_sm,
+    dq_hbm, dk_hbm, dv_hbm, gr_hbm, gp_hbm,
+    q_in, c_in, k_in, v_in, w_in, r_in, starts_in, owners_in, in_sem,
+    KV, Q, C2, WR, MB, P, HT, GH, PL,
+    dq_out, dk_out, dv_out, grad_out, out_sem, DQ,
     halo_send, halo_recv,
     SB, RB, OWN, back_send, back_recv,
     G, R1, one_send, one_recv,
@@ -135,10 +137,14 @@
     def there(x):
         return (rep, x)
 
+    row_first = ctx * 128
+    lanes = pl.ds(pl.multiple_of(row_first, 128), 128)
     loads = []
-    for i, (src, dst) in enumerate(
-        ((k_hbm, k_in), (v_hbm, v_in), (q_hbm, q_in), (c_hbm, c_in), (w_hbm, w_in), (r_hbm, r_in))
-    ):
+    for i, (src, dst) in enumerate((
+        (k_hbm, k_in), (v_hbm, v_in),
+        (starts_hbm.at[:, lanes], starts_in), (owners_hbm.at[:, lanes], owners_in),
+        (q_hbm, q_in), (c_hbm, c_in), (w_hbm, w_in), (r_hbm, r_in),
+    )):
         cp = pltpu.make_async_copy(src, dst, in_sem.at[i])
         cp.start()
         loads.append(cp)
@@ -162,15 +168,11 @@
     for m in range(4):
         KV[m, 0, HALO:] = kk[m]
         KV[m, 1, HALO:] = vv[m]
-    loads[2].wait()
-    loads[3].wait()
-    loads[4].wait()
-    loads[5].wait()
+    for cp in loads[2:]:
+        cp.wait()
     stage_prep(q_in, c_in, w_in, r_in, Q, C2, WR)
-    row_first = ctx * 128
-    lanes = pl.ds(pl.multiple_of(row_first, 128), 128)
-    own = owners_ref[:, lanes]
-    stage_mask(starts_ref[:, lanes], row_first, MB)
+    own = owners_in[...]
+    stage_mask(starts_in[...], row_first, MB)
 
     pl.semaphore_wait(barrier, 2 + (CHIPS - 1) + (REPS - 1))
 
@@ -267,22 +269,35 @@
 
     lax.fori_loop(0, 4, bwd, 0)
 
-    for m in range(4):
-        dq_ref[:, 8 * m : 8 * m + 8, :] = jnp.swapaxes(DQ[8 * m : 8 * m + 8], 0, 1)
+    stores = []
+    for m in range(4):
+        heads = slice(8 * m, 8 * m + 8)
+        dq_out[:, heads, :] = jnp.swapaxes(DQ[heads], 0, 1)
+        cp = pltpu.make_async_copy(dq_out.at[:, heads], dq_hbm.at[:, heads], out_sem.at[m])
+        cp.start()
+        stores.append(cp)
 
     mine = S3[rep]
     for d in range(1, REPS):
         three_copy(d).wait_recv()
         mine = mine + R3[d]
-    gr_ref[...] = mine[0:4]
-    gp_ref[...] = mine[4:8]
+    grad_out[0] = mine[0:4]
+    grad_out[1] = mine[4:8]
+    for i, dst in enumerate((gr_hbm, gp_hbm)):
+        cp = pltpu.make_async_copy(grad_out.at[i], dst, out_sem.at[4 + i])
+        cp.start()
+        stores.append(cp)
 
     for m in range(4):
         for s in (1, 2):
             back_copy(m, s).wait_recv()
     total = OWN[...] + RB[:, 0].astype(f32) + RB[:, 1].astype(f32)
-    dk_ref[...] = jnp.swapaxes(total[:, 0], 0, 1).astype(bf16)
-    dv_ref[...] = jnp.swapaxes(total[:, 1], 0, 1).astype(bf16)
+    dk_out[...] = jnp.swapaxes(total[:, 0], 0, 1).astype(bf16)
+    dv_out[...] = jnp.swapaxes(total[:, 1], 0, 1).astype(bf16)
+    for i, (src, dst) in enumerate(((dk_out, dk_hbm), (dv_out, dv_hbm))):
+        cp = pltpu.make_async_copy(src, dst, out_sem.at[6 + i])
+        cp.start()
+        stores.append(cp)
 
     for m in range(4):
         one_copy(m).wait_send()
@@ -293,33 +308,55 @@
         two_copy(d).wait_send()
     for d in range(1, REPS):
         three_copy(d).wait_send()
+    for cp in stores:
+        cp.wait()
+
+
+def finish(*refs):
+    srcs, dsts, bufs, sems = refs[:5], refs[5:10], refs[10:15], refs[15]
+    moves = [(srcs[i], bufs[i], dsts[i]) for i in range(1, 5)]
+    for i in range(4):
+        rows = pl.ds(32 * i, 32)
+        moves.append((srcs[0].at[rows], bufs[0].at[rows], dsts[0].at[rows]))
+    loads, stores = [], []
+    for i, (src, buf, dst) in enumerate(moves):
+        loads.append(pltpu.make_async_copy(src, buf, sems.at[0, i]))
+        stores.append(pltpu.make_async_copy(buf, dst, sems.at[1, i]))
+        loads[i].start()
+    for load, store in zip(loads, stores):
+        load.wait()
+        store.start()
+    for store in stores:
+        store.wait()
 
 
 def on_device(
     query_rows, key_rows, value_matrix, cotangent, rotation, projection, shift_bias,
     doc_starts, tenant_ids,
 ):
-    vmem = pl.BlockSpec(memory_space=pltpu.VMEM)
     smem = pl.BlockSpec(memory_space=pltpu.SMEM)
-    hbm = pl.BlockSpec(memory_space=pl.ANY)
+    hbm = pl.BlockSpec(memory_space=pltpu.HBM)
     dma = pltpu.SemaphoreType.DMA
     rows = (128, 32, 128)
+    kv_rows = (128, 4, 128)
+    out_shape = (
+        jax.ShapeDtypeStruct(rows, bf16),
+        jax.ShapeDtypeStruct(kv_rows, bf16),
+        jax.ShapeDtypeStruct(kv_rows, bf16),
+        jax.ShapeDtypeStruct((4, 128), f32),
+        jax.ShapeDtypeStruct((4, 128), f32),
+    )
     out = pl.pallas_call(
         kernel,
-        out_shape=(
-            jax.ShapeDtypeStruct(rows, bf16),
-            jax.ShapeDtypeStruct((128, 4, 128), bf16),
-            jax.ShapeDtypeStruct((128, 4, 128), bf16),
-            jax.ShapeDtypeStruct((4, 128), f32),
-            jax.ShapeDtypeStruct((4, 128), f32),
-        ),
-        in_specs=[hbm] * 6 + [smem, vmem, vmem],
-        out_specs=(vmem,) * 5,
+        out_shape=out_shape,
+        in_specs=[hbm] * 8 + [smem],
+        out_specs=(hbm,) * 5,
         scratch_shapes=[
             pltpu.VMEM(rows, bf16), pltpu.VMEM(rows, bf16),
             pltpu.VMEM((128, 4, 128), bf16), pltpu.VMEM((128, 4, 128), bf16),
             pltpu.VMEM((64, 32, 128), bf16), pltpu.VMEM((64, 32, 128), bf16),
-            dma((6,)),
+            pltpu.VMEM((1, 128), jnp.int32), pltpu.VMEM((1, 128), jnp.int32),
+            dma((8,)),
             pltpu.VMEM((4, 2, 384, 128), bf16),
             pltpu.VMEM((4, 1024, 128), bf16),
             pltpu.VMEM((128, 4096), bf16),
@@ -328,8 +365,10 @@
             pltpu.VMEM((4, 384, 1024), bf16),
             pltpu.VMEM((4096, 128), bf16),
             pltpu.VMEM((4, 1024, 128), bf16),
+            pltpu.VMEM((64, 128), bf16),
+            pltpu.VMEM(rows, bf16), pltpu.VMEM((128, 4, 128), bf16), pltpu.VMEM((128, 4, 128), bf16),
+            pltpu.VMEM((2, 4, 128), f32), dma((8,)),
             pltpu.VMEM((32, 128, 128), bf16),
-            pltpu.VMEM((64, 128), bf16),
             dma((4, 2)), dma((4, 2)),
             pltpu.VMEM((4, 2, 2, 128, 128), bf16),
             pltpu.VMEM((4, 2, 2, 128, 128), bf16),
@@ -346,15 +385,23 @@
             dma((REPS,)), dma((REPS,)),
         ],
         compiler_params=pltpu.CompilerParams(
-            collective_id=0, has_side_effects=True, vmem_limit_bytes=48 << 20
+            collective_id=0, has_side_effects=True, vmem_limit_bytes=VMEM_LIMIT
         ),
         name="steered_attention_backward",
     )(
         query_rows[0], cotangent[0], key_rows[0], value_matrix[0],
         projection.reshape(64, 32, 128), rotation.reshape(64, 32, 128),
-        shift_bias, doc_starts, tenant_ids,
+        doc_starts, tenant_ids, shift_bias.T,
     )
-    dq, dk, dv, gr, gp = out
+    dq, dk, dv, gr, gp = pl.pallas_call(
+        finish,
+        out_shape=out_shape,
+        in_specs=[hbm] * 5,
+        out_specs=(hbm,) * 5,
+        scratch_shapes=[pltpu.VMEM(s.shape, s.dtype) for s in out_shape] + [dma((2, 8))],
+        compiler_params=pltpu.CompilerParams(vmem_limit_bytes=VMEM_LIMIT),
+        name="finish",
+    )(*out)
     return dq[None], dk[None], dv[None], gr.reshape(1, 4, 1, 128), gp.reshape(1, 4, 1, 128)
 
 

time: 62.6 us -> 53.4 us (0.85)
  local copies, waits for them, and re-layouts: 11.3 us -> 0 us
  Pallas kernels: 50.2 us -> 52.6 us
    unnamed x22 -> x0, local copies, waits for them, and re-layouts: 11.3 us -> none
    pallas_call x1 -> x2, Pallas kernels: 50.2 us -> 52.6 us  [the longest x1 50.4 us: on_device(): pl.pallas_call(kernel, out_shape=out_shape, in_specs=[hbm] * 8 + [smem],...]
where the time goes in v2:
time: 53.4 us; the launch traced here: 53.2 us
  Pallas kernels  52.6 us (99%)
  between operations  0.64 us (1%)
    pallas_call x1, Pallas kernels, on_device(): pl.pallas_call(kernel, out_shape=out_shape, in_specs=[hbm] * 8 + [smem],...  50.4 us
    pallas_call x1, Pallas kernels, on_device(): pl.pallas_call(finish, out_shape=out_shape, in_specs=[hbm] * 5, out_specs...  2.2 us

profile of v2, /device:TPU:30, one launch (start us, length us, event | category | flops | bytes accessed | tf_op | source)
XLA Modules:
  0.0 53.2 jit_solution(1437314085540750219)
XLA Ops:
  0.6 50.4 %steered_attention_backward.1 = (bf16[128,32,128]{2,1,0:T(8,128)(2,1)}, bf16[128,4,128]{2,1,0:T(4,128)(2,1)}, bf16[128,4,128]{2,1,0:T(4,128)(2,1)}, f32[4,128]{1,0:T(4,128)}, f32[4,128]{1,0:T(4,128)}) custom-call(bf16[128,32,128]{2,1,0:T(8,128)(2,1)} %bitcast.16, bf16[128,32,128]{2,1,0:T(8,128)(2,1)} %bitcast.17, bf16[128,4,128]{2,1,0:T(4,128)(2,1)} %bitcast.20, ...), custom_call_target="tpu_custom_call" | custom-call | tf_op jit(solution)/shard_map/steered_attention_backward/pallas_call | solution.py:349
  51.0 2.2 %finish.1 = (bf16[128,32,128]{2,1,0:T(8,128)(2,1)}, bf16[128,4,128]{2,1,0:T(4,128)(2,1)}, bf16[128,4,128]{2,1,0:T(4,128)(2,1)}, f32[4,128]{1,0:T(4,128)}, f32[4,128]{1,0:T(4,128)}) custom-call(bf16[128,32,128]{2,1,0:T(8,128)(2,1)} %get-tuple-element.15.refs_0_, bf16[128,4,128]{2,1,0:T(4,128)(2,1)} %get-tuple-element.16.refs_1_, ...), custom_call_target="tpu_custom_call" | custom-call | tf_op jit(solution)/shard_map/finish/pallas_call | solution.py:396

commit v3 on v2

--- a/solution.py
+++ b/solution.py
@@ -49,10 +49,11 @@
         HT[pl.ds(m * 1024 + g * 128, 128), :] = ht[:, g * 128 : (g + 1) * 128]
 
 
-def stage_pull(own, WR, C2, GH, PL):
+def stage_pull(own, WR, C2, GH, PP):
     mask = iota((64, 128), 0) // 4 == own
     pull = jnp.where(mask, dot_nt(WR[64:128], C2[...]), 0.0)
-    PL[...] = pull.astype(bf16)
+    swap = iota((64, 64), 1) == (iota((64, 64), 0) ^ 4)
+    PP[...] = dot(jnp.where(swap, 1.0, 0.0).astype(bf16), pull.astype(bf16)).astype(bf16)
     pt = jnp.concatenate([pull, -pull], axis=0).T.astype(bf16)
     for m in range(4):
         cols = slice(m * 1024, (m + 1) * 1024)
@@ -61,9 +62,20 @@
             GH[m, g * 128 : (g + 1) * 128, :] = gh[:, g * 128 : (g + 1) * 128]
 
 
-def stage_tenant(own, bias_sm, WR, C2, HT, PL, G, send):
+def split_heads(part, m, G):
+    part = part.astype(bf16)
+    for g in range(8):
+        G[g % 2, m * 4 + g // 2] = part[:, g * 128 : (g + 1) * 128]
+
+
+def stage_projection(m, WR, HT, PP, LIFT, G):
+    hidden = HT[pl.ds(m * 1024, 1024), :]
+    LIFT[...] += dot(WR[:, pl.ds(pl.multiple_of(m * 1024, 1024), 1024)], hidden)
+    split_heads(dot_nt(PP[...], hidden), m, G)
+
+
+def stage_rotation(own, bias_sm, C2, LIFT, G, send):
     mask = iota((64, 128), 0) // 4 == own
-    lift2 = dot(WR[...], HT[...])
     ridx = iota((8, 128), 0)
     shifts = []
     for b in range(8):
@@ -71,20 +83,10 @@
         for r in range(8):
             a = jnp.where(ridx == r, bias_sm[r % 4, (b * 8 + r) // 4], a)
         shifts.append(a)
-    lift = lift2[0:64] - lift2[64:128] + jnp.concatenate(shifts, axis=0)
+    lift = LIFT[0:64] - LIFT[64:128] + jnp.concatenate(shifts, axis=0)
     lift = jnp.where(mask, lift, 0.0).astype(bf16)
-    r = iota((128, 64), 0)
-    c = iota((128, 64), 1)
-    hit = c == (r // 8) * 4 + r % 4
-    first = (r // 4) % 2 == 0
-    li = dot(jnp.where(hit & first, 1.0, 0.0).astype(bf16), lift).astype(bf16)
-    pi = dot(jnp.where(hit, jnp.where(first, -1.0, 1.0), 0.0).astype(bf16), PL[...]).astype(bf16)
-    for m in range(4):
-        part = dot(li, C2[:, m * 1024 : (m + 1) * 1024])
-        part = part + dot_nt(pi, HT[m * 1024 : (m + 1) * 1024, :])
-        part = part.astype(bf16)
-        for g in range(8):
-            G[g % 2, m * 4 + g // 2] = part[:, g * 128 : (g + 1) * 128]
+    for m in range(4):
+        split_heads(dot(lift, C2[:, m * 1024 : (m + 1) * 1024]), m, G)
         send(m)
 
 
@@ -119,9 +121,9 @@
     q_hbm, c_hbm, k_hbm, v_hbm, w_hbm, r_hbm, starts_hbm, owners_hbm, bias_sm,
     dq_hbm, dk_hbm, dv_hbm, gr_hbm, gp_hbm,
     q_in, c_in, k_in, v_in, w_in, r_in, starts_in, owners_in, in_sem,
-    KV, Q, C2, WR, MB, P, HT, GH, PL,
+    KV, Q, C2, WR, MB, P, HT, GH, PP, LIFT,
     dq_out, dk_out, dv_out, grad_out, out_sem, DQ,
-    halo_send, halo_recv,
+    halo_send, halo_recv, met,
     SB, RB, OWN, back_send, back_recv,
     G, R1, one_send, one_recv,
     S2, R2, two_send, two_recv,
@@ -150,16 +152,17 @@
         loads.append(cp)
 
     barrier = pltpu.get_barrier_semaphore()
-    for d in (1, CTXS - 1):
+    for d in [1, CTXS - 1] + list(range(2, CTXS, 2)):
         pl.semaphore_signal(barrier, inc=1, device_id=there((ctx + d) % CTXS), device_id_type=MESH)
-    for d in range(1, CHIPS):
-        pl.semaphore_signal(
-            barrier, inc=1, device_id=there((ctx + 2 * d) % CTXS), device_id_type=MESH
-        )
-    for d in range(1, REPS):
-        pl.semaphore_signal(
-            barrier, inc=1, device_id=((rep + d) % REPS, ctx), device_id_type=MESH
-        )
+
+    def along_z(d):
+        return ((rep + d) % REPS, ctx)
+
+    def greet_z(sem, d):
+        for x in (d, REPS - d):
+            pl.semaphore_signal(sem, inc=1, device_id=along_z(x), device_id_type=MESH)
+
+    greet_z(barrier, 1)
 
     loads[0].wait()
     loads[1].wait()
@@ -168,44 +171,53 @@
     for m in range(4):
         KV[m, 0, HALO:] = kk[m]
         KV[m, 1, HALO:] = vv[m]
+    pl.semaphore_wait(barrier, 2 + (CHIPS - 1) + 2)
+    greet_z(met.at[0], 1)
+
+    def far_copy(m):
+        return pltpu.make_async_remote_copy(
+            src_ref=KV.at[m, :, pl.ds(HALO, 128)],
+            dst_ref=KV.at[m, :, pl.ds(0, 128)],
+            send_sem=halo_send.at[m, 1],
+            recv_sem=halo_recv.at[m, 1],
+            device_id=there((ctx + 2) % CTXS),
+            device_id_type=MESH,
+        )
+
+    def near_copy(m):
+        return pltpu.make_async_remote_copy(
+            src_ref=KV.at[m, :, pl.ds(pl.multiple_of(HALO * (1 - core), 128), 128)],
+            dst_ref=KV.at[m, :, pl.ds(128, 128)],
+            send_sem=halo_send.at[m, 0],
+            recv_sem=halo_recv.at[m, 0],
+            device_id=there(mate),
+            device_id_type=MESH,
+        )
+
+    for m in range(4):
+        far_copy(m).start()
+
+    @pl.when(core == 0)
+    def _():
+        for m in range(4):
+            near_copy(m).start()
+
     for cp in loads[2:]:
         cp.wait()
     stage_prep(q_in, c_in, w_in, r_in, Q, C2, WR)
     own = owners_in[...]
     stage_mask(starts_in[...], row_first, MB)
-
-    pl.semaphore_wait(barrier, 2 + (CHIPS - 1) + (REPS - 1))
-
-    def halo_copy(m, s):
-        return pltpu.make_async_remote_copy(
-            src_ref=KV.at[m, :, pl.ds(HALO, 128)],
-            dst_ref=KV.at[m, :, pl.ds(HALO - 128 * s, 128)],
-            send_sem=halo_send.at[m, s - 1],
-            recv_sem=halo_recv.at[m, s - 1],
-            device_id=there((ctx + s) % CTXS),
-            device_id_type=MESH,
-        )
-
-    for m in range(4):
-        for s in (1, 2):
-            halo_copy(m, s).start()
-
-    stage_pull(own, WR, C2, GH, PL)
-
-    def fwd(m, carry):
-        for s in (1, 2):
-            halo_copy(m, s).wait_recv()
-        stage_fwd(m, KV, Q, MB, P, HT, scale)
-        return carry
-
-    lax.fori_loop(0, 4, fwd, 0)
-
-    def one_copy(m):
-        return pltpu.make_async_remote_copy(
-            src_ref=G.at[1 - core, pl.ds(4 * m, 4)],
-            dst_ref=R1.at[pl.ds(4 * m, 4)],
-            send_sem=one_send.at[m],
-            recv_sem=one_recv.at[m],
+    stage_pull(own, WR, C2, GH, PP)
+    LIFT[...] = jnp.zeros_like(LIFT)
+    pl.semaphore_wait(met.at[0], 2)
+    greet_z(met.at[1], 2)
+
+    def one_copy(p, m):
+        return pltpu.make_async_remote_copy(
+            src_ref=G.at[p, 1 - core, pl.ds(4 * m, 4)],
+            dst_ref=R1.at[p, pl.ds(4 * m, 4)],
+            send_sem=one_send.at[p, m],
+            recv_sem=one_recv.at[p, m],
             device_id=there(mate),
             device_id_type=MESH,
         )
@@ -220,15 +232,45 @@
             device_id_type=MESH,
         )
 
+    def pair_sum(p, m):
+        one_copy(p, m).wait_recv()
+        part = pl.ds(4 * m, 4)
+        S2[part, p] = (G[p, core, part].astype(f32) + R1[p, part].astype(f32)).astype(bf16)
+
+    def chip_sum():
+        total = S2[chip].astype(f32)
+        for d in range(1, CHIPS):
+            two_copy(d).wait_recv()
+            total = total + R2[d].astype(f32)
+        return total[0], total[1]
+
     def three_copy(d):
         return pltpu.make_async_remote_copy(
             src_ref=S3.at[(rep + d) % REPS],
             dst_ref=R3.at[d],
             send_sem=three_send.at[d],
             recv_sem=three_recv.at[d],
-            device_id=((rep + d) % REPS, ctx),
-            device_id_type=MESH,
-        )
+            device_id=along_z(d),
+            device_id_type=MESH,
+        )
+
+    def fwd(m, carry):
+        far_copy(m).wait_recv()
+
+        @pl.when(core == 1)
+        def _():
+            near_copy(m).start()
+
+        near_copy(m).wait_recv()
+        stage_fwd(m, KV, Q, MB, P, HT, scale)
+        stage_projection(m, WR, HT, PP, LIFT, G.at[1])
+        one_copy(1, m).start()
+
+        return carry
+
+    lax.fori_loop(0, 4, fwd, 0)
+    pl.semaphore_wait(met.at[1], 2)
+    greet_z(met.at[2], 4)
 
     def back_copy(m, s):
         return pltpu.make_async_remote_copy(
@@ -240,51 +282,40 @@
             device_id_type=MESH,
         )
 
-    stage_tenant(own, bias_sm, WR, C2, HT, PL, G, lambda m: one_copy(m).start())
+    stage_rotation(own, bias_sm, C2, LIFT, G.at[0], lambda m: one_copy(0, m).start())
+    for m in range(4):
+        pair_sum(1, m)
 
     def bwd(m, carry):
         stage_bwd(m, KV, Q, P, GH, scale, DQ, SB, OWN)
-        for s in (1, 2):
-            back_copy(m, s).start()
 
         @pl.when(m == 0)
         def _():
             for i in range(4):
-                one_copy(i).wait_recv()
-            S2[...] = (G[core].astype(f32) + R1[...].astype(f32)).astype(bf16)
+                pair_sum(0, i)
             for d in range(1, CHIPS):
                 two_copy(d).start()
 
-        @pl.when(m == 2)
-        def _():
-            total = S2[chip].astype(f32)
-            for d in range(1, CHIPS):
-                two_copy(d).wait_recv()
-                total = total + R2[d].astype(f32)
-            S3[...] = total.reshape(REPS, 8, 128)
-            for d in range(1, REPS):
-                three_copy(d).start()
-
+        for s in (1, 2):
+            back_copy(m, s).start()
         return carry
 
     lax.fori_loop(0, 4, bwd, 0)
+    rot, proj = chip_sum()
+    upper = iota((8, 128), 0) < 4
+    for t in range(0, REPS, 2):
+        a, c = rot[4 * t : 4 * t + 8], proj[4 * t : 4 * t + 8]
+        S3[t] = jnp.where(upper, a, c)
+        S3[t + 1] = jnp.where(upper, c, a)
+    pl.semaphore_wait(met.at[2], 2)
+    for d in range(1, REPS):
+        three_copy(d).start()
 
     stores = []
     for m in range(4):
         heads = slice(8 * m, 8 * m + 8)
         dq_out[:, heads, :] = jnp.swapaxes(DQ[heads], 0, 1)
         cp = pltpu.make_async_copy(dq_out.at[:, heads], dq_hbm.at[:, heads], out_sem.at[m])
-        cp.start()
-        stores.append(cp)
-
-    mine = S3[rep]
-    for d in range(1, REPS):
-        three_copy(d).wait_recv()
-        mine = mine + R3[d]
-    grad_out[0] = mine[0:4]
-    grad_out[1] = mine[4:8]
-    for i, dst in enumerate((gr_hbm, gp_hbm)):
-        cp = pltpu.make_async_copy(grad_out.at[i], dst, out_sem.at[4 + i])
         cp.start()
         stores.append(cp)
 
@@ -299,10 +330,26 @@
         cp.start()
         stores.append(cp)
 
-    for m in range(4):
-        one_copy(m).wait_send()
+    mine = S3[rep]
+    for d in range(1, REPS):
+        three_copy(d).wait_recv()
+        mine = mine + R3[d]
+    odd = rep % 2 == 1
+    low, high = mine[0:4], mine[4:8]
+    proj = jnp.where(odd, low, high)
+    grad_out[0] = jnp.where(odd, high, low) - proj
+    grad_out[1] = proj
+    for i, dst in enumerate((gr_hbm, gp_hbm)):
+        cp = pltpu.make_async_copy(grad_out.at[i], dst, out_sem.at[4 + i])
+        cp.start()
+        stores.append(cp)
+
+    for m in range(4):
+        one_copy(0, m).wait_send()
+        one_copy(1, m).wait_send()
+        far_copy(m).wait_send()
+        near_copy(m).wait_send()
         for s in (1, 2):
-            halo_copy(m, s).wait_send()
             back_copy(m, s).wait_send()
     for d in range(1, CHIPS):
         two_copy(d).wait_send()
@@ -366,19 +413,20 @@
             pltpu.VMEM((4096, 128), bf16),
             pltpu.VMEM((4, 1024, 128), bf16),
             pltpu.VMEM((64, 128), bf16),
+            pltpu.VMEM((128, 128), f32),
             pltpu.VMEM(rows, bf16), pltpu.VMEM((128, 4, 128), bf16), pltpu.VMEM((128, 4, 128), bf16),
             pltpu.VMEM((2, 4, 128), f32), dma((8,)),
             pltpu.VMEM((32, 128, 128), bf16),
-            dma((4, 2)), dma((4, 2)),
+            dma((4, 2)), dma((4, 2)), pltpu.SemaphoreType.REGULAR((3,)),
             pltpu.VMEM((4, 2, 2, 128, 128), bf16),
             pltpu.VMEM((4, 2, 2, 128, 128), bf16),
             pltpu.VMEM((4, 2, 128, 128), f32),
             dma((4, 2)), dma((4, 2)),
-            pltpu.VMEM((2, CHIPS, 128, 128), bf16),
-            pltpu.VMEM((CHIPS, 128, 128), bf16),
-            dma((4,)), dma((4,)),
-            pltpu.VMEM((CHIPS, 128, 128), bf16),
-            pltpu.VMEM((CHIPS, 128, 128), bf16),
+            pltpu.VMEM((2, 2, CHIPS, 64, 128), bf16),
+            pltpu.VMEM((2, CHIPS, 64, 128), bf16),
+            dma((2, 4)), dma((2, 4)),
+            pltpu.VMEM((CHIPS, 2, 64, 128), bf16),
+            pltpu.VMEM((CHIPS, 2, 64, 128), bf16),
             dma((CHIPS,)), dma((CHIPS,)),
             pltpu.VMEM((REPS, 8, 128), f32),
             pltpu.VMEM((REPS, 8, 128), f32),

time: 53.4 us -> 49.3 us (0.923)
  the two profiles are of different devices: /device:TPU:30 before, /device:TPU:24 now
where the time goes in v3:
time: 49.3 us; the launch traced here: 49.1 us
  Pallas kernels  48.5 us (98%)
  between operations  0.64 us (1%)
    pallas_call x1, Pallas kernels, on_device(): pl.pallas_call(kernel, out_shape=out_shape, in_specs=[hbm] * 8 + [smem],...  46.3 us
    pallas_call x1, Pallas kernels, on_device(): pl.pallas_call(finish, out_shape=out_shape, in_specs=[hbm] * 5, out_specs...  2.2 us

profile of v3, /device:TPU:24, one launch (start us, length us, event | category | flops | bytes accessed | tf_op | source)
XLA Modules:
  0.0 49.1 jit_solution(4739555322690427351)
XLA Ops:
  0.6 46.3 %steered_attention_backward.1 = (bf16[128,32,128]{2,1,0:T(8,128)(2,1)}, bf16[128,4,128]{2,1,0:T(4,128)(2,1)}, bf16[128,4,128]{2,1,0:T(4,128)(2,1)}, f32[4,128]{1,0:T(4,128)}, f32[4,128]{1,0:T(4,128)}) custom-call(bf16[128,32,128]{2,1,0:T(8,128)(2,1)} %bitcast.16, bf16[128,32,128]{2,1,0:T(8,128)(2,1)} %bitcast.17, bf16[128,4,128]{2,1,0:T(4,128)(2,1)} %bitcast.20, ...), custom_call_target="tpu_custom_call" | custom-call | tf_op jit(solution)/shard_map/steered_attention_backward/pallas_call | solution.py:396
  46.9 2.2 %finish.1 = (bf16[128,32,128]{2,1,0:T(8,128)(2,1)}, bf16[128,4,128]{2,1,0:T(4,128)(2,1)}, bf16[128,4,128]{2,1,0:T(4,128)(2,1)}, f32[4,128]{1,0:T(4,128)}, f32[4,128]{1,0:T(4,128)}) custom-call(bf16[128,32,128]{2,1,0:T(8,128)(2,1)} %get-tuple-element.15.refs_0_, bf16[128,4,128]{2,1,0:T(4,128)(2,1)} %get-tuple-element.16.refs_1_, ...), custom_call_target="tpu_custom_call" | custom-call | tf_op jit(solution)/shard_map/finish/pallas_call | solution.py:444

commit v4 on v3

--- a/solution.py
+++ b/solution.py
@@ -49,12 +49,16 @@
         HT[pl.ds(m * 1024 + g * 128, 128), :] = ht[:, g * 128 : (g + 1) * 128]
 
 
-def stage_pull(own, WR, C2, GH, PP):
+def stage_pull(own, WR, C2, PP, PT):
     mask = iota((64, 128), 0) // 4 == own
     pull = jnp.where(mask, dot_nt(WR[64:128], C2[...]), 0.0)
     swap = iota((64, 64), 1) == (iota((64, 64), 0) ^ 4)
     PP[...] = dot(jnp.where(swap, 1.0, 0.0).astype(bf16), pull.astype(bf16)).astype(bf16)
-    pt = jnp.concatenate([pull, -pull], axis=0).T.astype(bf16)
+    PT[...] = jnp.concatenate([pull, -pull], axis=0).T.astype(bf16)
+
+
+def stage_grad_hidden(WR, C2, PT, GH):
+    pt = PT[...]
     for m in range(4):
         cols = slice(m * 1024, (m + 1) * 1024)
         gh = (dot(pt, WR[:, cols]) + C2[:, cols].astype(f32)).astype(bf16)
@@ -121,7 +125,7 @@
     q_hbm, c_hbm, k_hbm, v_hbm, w_hbm, r_hbm, starts_hbm, owners_hbm, bias_sm,
     dq_hbm, dk_hbm, dv_hbm, gr_hbm, gp_hbm,
     q_in, c_in, k_in, v_in, w_in, r_in, starts_in, owners_in, in_sem,
-    KV, Q, C2, WR, MB, P, HT, GH, PP, LIFT,
+    KV, Q, C2, WR, MB, P, HT, GH, PP, PT, LIFT,
     dq_out, dk_out, dv_out, grad_out, out_sem, DQ,
     halo_send, halo_recv, met,
     SB, RB, OWN, back_send, back_recv,
@@ -207,7 +211,7 @@
     stage_prep(q_in, c_in, w_in, r_in, Q, C2, WR)
     own = owners_in[...]
     stage_mask(starts_in[...], row_first, MB)
-    stage_pull(own, WR, C2, GH, PP)
+    stage_pull(own, WR, C2, PP, PT)
     LIFT[...] = jnp.zeros_like(LIFT)
     pl.semaphore_wait(met.at[0], 2)
     greet_z(met.at[1], 2)
@@ -222,12 +226,12 @@
             device_id_type=MESH,
         )
 
-    def two_copy(d):
-        return pltpu.make_async_remote_copy(
-            src_ref=S2.at[(chip + d) % CHIPS],
-            dst_ref=R2.at[d],
-            send_sem=two_send.at[d],
-            recv_sem=two_recv.at[d],
+    def two_copy(p, d):
+        return pltpu.make_async_remote_copy(
+            src_ref=S2.at[p, (chip + d) % CHIPS],
+            dst_ref=R2.at[p, d],
+            send_sem=two_send.at[p, d],
+            recv_sem=two_recv.at[p, d],
             device_id=there((ctx + 2 * d) % CTXS),
             device_id_type=MESH,
         )
@@ -235,14 +239,31 @@
     def pair_sum(p, m):
         one_copy(p, m).wait_recv()
         part = pl.ds(4 * m, 4)
-        S2[part, p] = (G[p, core, part].astype(f32) + R1[p, part].astype(f32)).astype(bf16)
-
-    def chip_sum():
-        total = S2[chip].astype(f32)
+        S2[p, part] = (G[p, core, part].astype(f32) + R1[p, part].astype(f32)).astype(bf16)
+        for i in range(4):
+            d = (4 * m + i + CHIPS - chip) % CHIPS
+
+            @pl.when(d > 0)
+            def _():
+                two_copy(p, d).start()
+
+    def chip_sum(p):
+        total = S2[p, chip].astype(f32)
         for d in range(1, CHIPS):
-            two_copy(d).wait_recv()
-            total = total + R2[d].astype(f32)
-        return total[0], total[1]
+            two_copy(p, d).wait_recv()
+            total = total + R2[p, d].astype(f32)
+        return total
+
+    def spread():
+        proj, rot = chip_sum(1), chip_sum(0)
+        upper = iota((8, 128), 0) < 4
+        for t in range(0, REPS, 2):
+            a, c = rot[4 * t : 4 * t + 8], proj[4 * t : 4 * t + 8]
+            S3[t] = jnp.where(upper, a, c)
+            S3[t + 1] = jnp.where(upper, c, a)
+        pl.semaphore_wait(met.at[2], 2)
+        for d in range(1, REPS):
+            three_copy(d).start()
 
     def three_copy(d):
         return pltpu.make_async_remote_copy(
@@ -282,34 +303,23 @@
             device_id_type=MESH,
         )
 
+    for m in range(3):
+        pair_sum(1, m)
     stage_rotation(own, bias_sm, C2, LIFT, G.at[0], lambda m: one_copy(0, m).start())
-    for m in range(4):
-        pair_sum(1, m)
+    pair_sum(1, 3)
+    stage_grad_hidden(WR, C2, PT, GH)
+    for m in range(4):
+        pair_sum(0, m)
 
     def bwd(m, carry):
         stage_bwd(m, KV, Q, P, GH, scale, DQ, SB, OWN)
-
-        @pl.when(m == 0)
-        def _():
-            for i in range(4):
-                pair_sum(0, i)
-            for d in range(1, CHIPS):
-                two_copy(d).start()
 
         for s in (1, 2):
             back_copy(m, s).start()
         return carry
 
     lax.fori_loop(0, 4, bwd, 0)
-    rot, proj = chip_sum()
-    upper = iota((8, 128), 0) < 4
-    for t in range(0, REPS, 2):
-        a, c = rot[4 * t : 4 * t + 8], proj[4 * t : 4 * t + 8]
-        S3[t] = jnp.where(upper, a, c)
-        S3[t + 1] = jnp.where(upper, c, a)
-    pl.semaphore_wait(met.at[2], 2)
-    for d in range(1, REPS):
-        three_copy(d).start()
+    spread()
 
     stores = []
     for m in range(4):
@@ -352,7 +362,8 @@
         for s in (1, 2):
             back_copy(m, s).wait_send()
     for d in range(1, CHIPS):
-        two_copy(d).wait_send()
+        two_copy(0, d).wait_send()
+        two_copy(1, d).wait_send()
     for d in range(1, REPS):
         three_copy(d).wait_send()
     for cp in stores:
@@ -413,6 +424,7 @@
             pltpu.VMEM((4096, 128), bf16),
             pltpu.VMEM((4, 1024, 128), bf16),
             pltpu.VMEM((64, 128), bf16),
+            pltpu.VMEM((128, 128), bf16),
             pltpu.VMEM((128, 128), f32),
             pltpu.VMEM(rows, bf16), pltpu.VMEM((128, 4, 128), bf16), pltpu.VMEM((128, 4, 128), bf16),
             pltpu.VMEM((2, 4, 128), f32), dma((8,)),
@@ -425,9 +437,9 @@
             pltpu.VMEM((2, 2, CHIPS, 64, 128), bf16),
             pltpu.VMEM((2, CHIPS, 64, 128), bf16),
             dma((2, 4)), dma((2, 4)),
-            pltpu.VMEM((CHIPS, 2, 64, 128), bf16),
-            pltpu.VMEM((CHIPS, 2, 64, 128), bf16),
-            dma((CHIPS,)), dma((CHIPS,)),
+            pltpu.VMEM((2, CHIPS, 64, 128), bf16),
+            pltpu.VMEM((2, CHIPS, 64, 128), bf16),
+            dma((2, CHIPS)), dma((2, CHIPS)),
             pltpu.VMEM((REPS, 8, 128), f32),
             pltpu.VMEM((REPS, 8, 128), f32),
             dma((REPS,)), dma((REPS,)),

time: 49.3 us -> 46.3 us (0.939)
  the two profiles are of different devices: /device:TPU:24 before, /device:TPU:30 now
where the time goes in v4:
time: 46.3 us; the launch traced here: 46.2 us
  Pallas kernels  45.5 us (98%)
  between operations  0.64 us (1%)
    pallas_call x1, Pallas kernels, on_device(): pl.pallas_call(kernel, out_shape=out_shape, in_specs=[hbm] * 8 + [smem],...  43.3 us
    pallas_call x1, Pallas kernels, on_device(): pl.pallas_call(finish, out_shape=out_shape, in_specs=[hbm] * 5, out_specs...  2.2 us

profile of v4, /device:TPU:30, one launch (start us, length us, event | category | flops | bytes accessed | tf_op | source)
XLA Modules:
  0.0 46.2 jit_solution(5097666447681010841)
XLA Ops:
  0.6 43.3 %steered_attention_backward.1 = (bf16[128,32,128]{2,1,0:T(8,128)(2,1)}, bf16[128,4,128]{2,1,0:T(4,128)(2,1)}, bf16[128,4,128]{2,1,0:T(4,128)(2,1)}, f32[4,128]{1,0:T(4,128)}, f32[4,128]{1,0:T(4,128)}) custom-call(bf16[128,32,128]{2,1,0:T(8,128)(2,1)} %bitcast.16, bf16[128,32,128]{2,1,0:T(8,128)(2,1)} %bitcast.17, bf16[128,4,128]{2,1,0:T(4,128)(2,1)} %bitcast.20, ...), custom_call_target="tpu_custom_call" | custom-call | tf_op jit(solution)/shard_map/steered_attention_backward/pallas_call | solution.py:407
  44.0 2.2 %finish.1 = (bf16[128,32,128]{2,1,0:T(8,128)(2,1)}, bf16[128,4,128]{2,1,0:T(4,128)(2,1)}, bf16[128,4,128]{2,1,0:T(4,128)(2,1)}, f32[4,128]{1,0:T(4,128)}, f32[4,128]{1,0:T(4,128)}) custom-call(bf16[128,32,128]{2,1,0:T(8,128)(2,1)} %get-tuple-element.15.refs_0_, bf16[128,4,128]{2,1,0:T(4,128)(2,1)} %get-tuple-element.16.refs_1_, ...), custom_call_target="tpu_custom_call" | custom-call | tf_op jit(solution)/shard_map/finish/pallas_call | solution.py:456

commit v5 on v4

--- a/solution.py
+++ b/solution.py
@@ -117,6 +117,7 @@
 
 
 REPS, CTXS, CHIPS = 16, 32, 16
+FARTHEST_FIRST = sorted(range(1, REPS), key=lambda d: -min(d, REPS - d))
 HALO = 256
 VMEM_LIMIT = 60 << 20
 
@@ -156,7 +157,7 @@
         loads.append(cp)
 
     barrier = pltpu.get_barrier_semaphore()
-    for d in [1, CTXS - 1] + list(range(2, CTXS, 2)):
+    for d in [2 * d for d in FARTHEST_FIRST] + [1, CTXS - 1]:
         pl.semaphore_signal(barrier, inc=1, device_id=there((ctx + d) % CTXS), device_id_type=MESH)
 
     def along_z(d):
@@ -262,7 +263,7 @@
             S3[t] = jnp.where(upper, a, c)
             S3[t + 1] = jnp.where(upper, c, a)
         pl.semaphore_wait(met.at[2], 2)
-        for d in range(1, REPS):
+        for d in FARTHEST_FIRST:
             three_copy(d).start()
 
     def three_copy(d):

time: 46.3 us -> 45.4 us (0.981)
  Pallas kernels: 45.5 us -> 44.6 us
    pallas_call x1, Pallas kernels: 43.3 us -> 42.4 us  [on_device(): pl.pallas_call(kernel, out_shape=out_shape, in_specs=[hbm] * 8 + [smem],...]
where the time goes in v5:
time: 45.4 us; the launch traced here: 45.3 us
  Pallas kernels  44.6 us (98%)
  between operations  0.64 us (1%)
    pallas_call x1, Pallas kernels, on_device(): pl.pallas_call(kernel, out_shape=out_shape, in_specs=[hbm] * 8 + [smem],...  42.4 us
    pallas_call x1, Pallas kernels, on_device(): pl.pallas_call(finish, out_shape=out_shape, in_specs=[hbm] * 5, out_specs...  2.2 us

profile of v5, /device:TPU:30, one launch (start us, length us, event | category | flops | bytes accessed | tf_op | source)
XLA Modules:
  0.0 45.3 jit_solution(16140860940952247147)
XLA Ops:
  0.6 42.4 %steered_attention_backward.1 = (bf16[128,32,128]{2,1,0:T(8,128)(2,1)}, bf16[128,4,128]{2,1,0:T(4,128)(2,1)}, bf16[128,4,128]{2,1,0:T(4,128)(2,1)}, f32[4,128]{1,0:T(4,128)}, f32[4,128]{1,0:T(4,128)}) custom-call(bf16[128,32,128]{2,1,0:T(8,128)(2,1)} %bitcast.16, bf16[128,32,128]{2,1,0:T(8,128)(2,1)} %bitcast.17, bf16[128,4,128]{2,1,0:T(4,128)(2,1)} %bitcast.20, ...), custom_call_target="tpu_custom_call" | custom-call | tf_op jit(solution)/shard_map/steered_attention_backward/pallas_call | solution.py:408
  43.1 2.2 %finish.1 = (bf16[128,32,128]{2,1,0:T(8,128)(2,1)}, bf16[128,4,128]{2,1,0:T(4,128)(2,1)}, bf16[128,4,128]{2,1,0:T(4,128)(2,1)}, f32[4,128]{1,0:T(4,128)}, f32[4,128]{1,0:T(4,128)}) custom-call(bf16[128,32,128]{2,1,0:T(8,128)(2,1)} %get-tuple-element.15.refs_0_, bf16[128,4,128]{2,1,0:T(4,128)(2,1)} %get-tuple-element.16.refs_1_, ...), custom_call_target="tpu_custom_call" | custom-call | tf_op jit(solution)/shard_map/finish/pallas_call | solution.py:457
